TPU v7x, 32 devices: a whole 2x2x4 slice. The times are simulated.
32 devices in a mesh: mem: 4 (over y, core), ctx: 8 (over z, x).
Axes of the slice: x: 2, y: 2, z: 4, core: 2. Of those that a mesh axis runs over, the one named last changes fastest.
Arguments:
- queries: bfloat16 [8, 512, 32, 128], P('ctx', 'mem'), may hold values from -6 to 6
- keys: bfloat16 [8, 512, 32, 128], P('ctx', 'mem'), may hold values from -6 to 6
- values: bfloat16 [8, 512, 32, 128], P('ctx', 'mem'), may hold values from -6 to 6
- log_decay: bfloat16 [8, 512, 32], P('ctx', 'mem'), may hold values from -1 to 0, as said below
- routes: int32 [8, 512, 2], P('ctx', 'mem'), may hold values from 0 to 3, all different within a row; in each aligned block of 128 rows (0 to 127, 128 to 255, ..., all dimensions but the last counted through in order) at most 72 rows name the same one
- route_weight: float32 [8, 512, 2], P('ctx', 'mem'), may hold values from 0.2 to 1
- gain: float32 [4096], replicated, may hold values from 0.25 to 1.75
Outputs:
- layer_out: bfloat16 [8, 512, 32, 128], P('ctx', 'mem')
Inputs may be any that keep to these rules, and one draw needn't show every extreme that they name: `routes`: A token's two memories differ. Among the tokens of one device (an aligned block of 128 tokens) no memory is named by more than 72 tokens, and in some such block a memory is named by exactly 72. `log_decay`: entries are negative.
All inputs are finite; a program needn't handle non-finite values.
Results may differ from a plain program's by a relative error of at most 0.015.
Values may be sent and summed in bfloat16 or wider, within the bound.
No kernel may reach another device: no remote copies, remote signals or barrier semaphores. Data moves between devices by JAX's collectives and lax.ppermute only.
A program may use at most 128 MiB of HBM per device.

v0:
```python
import math
import jax
import jax.numpy as jnp
from jax import lax
from jax.sharding import PartitionSpec as P


def as_sent(array):

    def short(part):
        return part.astype(jnp.bfloat16) if part.dtype == jnp.float32 else part

    return jax.tree.map(short, array)


def split_parts(matrix):
    high = matrix.astype(jnp.bfloat16)
    low = (matrix - high.astype(jnp.float32)).astype(jnp.bfloat16)
    return (high, low)


def head_norm(rows):
    square_mean = jnp.mean(rows * rows, axis=-1, keepdims=True)
    return rows * lax.rsqrt(square_mean + 1e-06)


def local_terms(keys_in, incoming_values, rates_in):
    running_decay = jnp.cumsum(rates_in.astype(jnp.float32), axis=0)
    total = running_decay[-1]
    retained_mask = jnp.exp(total[None, :] - running_decay)
    upper_scaled_state, lower_scaled_state = split_parts(
        keys_in.astype(jnp.float32) * retained_mask[:, :, None]
    )
    state_increment = jnp.einsum(
        "dyn,dye->yne", upper_scaled_state, incoming_values, preferred_element_type=jnp.float32
    )
    state_increment = state_increment + jnp.einsum(
        "dyn,dye->yne", lower_scaled_state, incoming_values, preferred_element_type=jnp.float32
    )
    return (running_decay, jnp.exp(total), state_increment)


def compose_rows(earlier, later):
    return (earlier[0] * later[0], later[0][..., None] * earlier[1] + later[1])


def incoming_state(decay_total, state_increment):
    heads = state_increment.shape[0]
    hdim = state_increment.shape[1]
    flat_rows = heads * hdim
    pieces = (
        lax.all_to_all(
            state_increment.reshape(1, flat_rows, hdim).astype(jnp.bfloat16),
            "ctx",
            split_axis=1,
            concat_axis=0,
            tiled=True,
        ).astype(jnp.float32),
        lax.all_to_all(
            jnp.repeat(decay_total, hdim).reshape(1, flat_rows).astype(jnp.bfloat16),
            "ctx",
            split_axis=1,
            concat_axis=0,
            tiled=True,
        ).astype(jnp.float32),
    )
    inclusive = lax.associative_scan(compose_rows, (pieces[1], pieces[0]), axis=0)
    shifted = jnp.concatenate([jnp.zeros_like(inclusive[1][:1]), inclusive[1][:-1]], axis=0)
    returned = lax.all_to_all(
        as_sent(shifted), "ctx", split_axis=0, concat_axis=1, tiled=True
    ).astype(shifted.dtype)
    return returned.reshape(heads, hdim, hdim)


def memory_readout(
    queries_in, keys_in, incoming_values, running_decay, entering_state, query_scale
):
    count_rows = queries_in.shape[0]
    heads = queries_in.shape[1]
    hdim = queries_in.shape[2]
    width = math.gcd(heads, 8)
    causal = jnp.arange(count_rows)[:, None] >= jnp.arange(count_rows)[None, :]

    def one_group(index, result):
        start = index * width
        query_group_rows = lax.dynamic_slice_in_dim(queries_in, start, width, 1)
        group_key = lax.dynamic_slice_in_dim(keys_in, start, width, 1)
        group_value = lax.dynamic_slice_in_dim(incoming_values, start, width, 1)
        group_cumul = lax.dynamic_slice_in_dim(running_decay, start, width, 1)
        group_state = lax.dynamic_slice_in_dim(entering_state, start, width, 0)
        head_cumul = group_cumul.T
        masked = jnp.where(causal, head_cumul[:, :, None] - head_cumul[:, None, :], -jnp.inf)
        scores = jnp.einsum(
            "ihd,jhd->hij", query_group_rows, group_key, preferred_element_type=jnp.float32
        )
        weights = (jnp.exp(masked) * scores * query_scale).astype(jnp.bfloat16)
        intra = jnp.einsum("hij,jhd->ihd", weights, group_value, preferred_element_type=jnp.float32)
        upper_state_part, lower_state_part = split_parts(group_state)
        across_block_output = jnp.einsum(
            "epm,pmx->epx", query_group_rows, upper_state_part, preferred_element_type=jnp.float32
        )
        across_block_output = across_block_output + jnp.einsum(
            "epm,pmx->epx", query_group_rows, lower_state_part, preferred_element_type=jnp.float32
        )
        across_block_output = across_block_output * (jnp.exp(group_cumul) * query_scale)[:, :, None]
        group_out = (intra + across_block_output).astype(jnp.bfloat16)
        return lax.dynamic_update_slice_in_dim(result, group_out, start, 1)

    return lax.fori_loop(
        0, heads // width, one_group, jnp.zeros((count_rows, heads, hdim), jnp.bfloat16)
    )


def shards(queries, keys, values, log_decay, routes, route_weight, gain):
    tokens_here = queries.shape[1]
    heads = queries.shape[2]
    hdim = queries.shape[3]
    memories = lax.axis_size("mem")
    capacity = 2 * tokens_here // memories + tokens_here // 16
    query_scale = hdim ** (-0.5)
    local_routes = routes[0]
    member = jnp.any(
        local_routes[:, :, None] == jnp.arange(memories, dtype=jnp.int32)[None, None, :], axis=1
    )
    counted = member.astype(jnp.int32)
    rank = jnp.cumsum(counted, axis=0) - counted
    match = member[None, :, :] & (
        rank[None, :, :] == jnp.arange(capacity, dtype=jnp.int32)[:, None, None]
    )
    source = jnp.sum(
        jnp.where(match, jnp.arange(tokens_here, dtype=jnp.int32)[None, :, None], 0), axis=1
    ).T.reshape(-1)
    filled = jnp.any(match, axis=1).T.reshape(-1)

    def packed(table):
        shaped = filled.reshape((-1,) + (1,) * (table.ndim - 1))
        rows_out = jnp.where(shaped, table[source], jnp.zeros((), table.dtype))
        return rows_out.reshape((memories, capacity) + table.shape[1:])

    query_send = packed(queries[0])
    key_send = packed(keys[0])
    value_send = packed(values[0])
    rate_send = packed(log_decay[0])
    count_rows = memories * capacity
    query_got, key_got, value_got, rate_got = (
        lax.all_to_all(query_send, "mem", split_axis=0, concat_axis=0, tiled=True),
        lax.all_to_all(key_send, "mem", split_axis=0, concat_axis=0, tiled=True),
        lax.all_to_all(value_send, "mem", split_axis=0, concat_axis=0, tiled=True),
        lax.all_to_all(rate_send, "mem", split_axis=0, concat_axis=0, tiled=True),
    )
    running_decay, decay_total, state_increment = local_terms(
        key_got.reshape(count_rows, heads, hdim),
        value_got.reshape(count_rows, heads, hdim),
        rate_got.reshape(count_rows, heads),
    )
    entering_state = incoming_state(decay_total, state_increment)
    readout = memory_readout(
        query_got.reshape(count_rows, heads, hdim),
        key_got.reshape(count_rows, heads, hdim),
        value_got.reshape(count_rows, heads, hdim),
        running_decay,
        entering_state,
        query_scale,
    )
    returned = lax.all_to_all(
        readout.reshape(memories, capacity, heads, hdim),
        "mem",
        split_axis=0,
        concat_axis=0,
        tiled=True,
    )
    flat = returned.reshape(count_rows, heads, hdim)
    picked_rank = jnp.take_along_axis(rank, local_routes, axis=1)
    slot_index = local_routes * capacity + picked_rank
    first_out = head_norm(flat[slot_index[:, 0]].astype(jnp.float32))
    second_out = head_norm(flat[slot_index[:, 1]].astype(jnp.float32))
    local_weight = route_weight[0]
    mixed = first_out * local_weight[:, 0, None, None] + second_out * local_weight[:, 1, None, None]
    return (mixed * gain.reshape(heads, hdim)).astype(jnp.bfloat16)[None]


def solution(mesh):
    return jax.shard_map(
        shards,
        mesh=mesh,
        in_specs=(
            P("ctx", "mem", None, None),
            P("ctx", "mem", None, None),
            P("ctx", "mem", None, None),
            P("ctx", "mem", None),
            P("ctx", "mem", None),
            P("ctx", "mem", None),
            P(),
        ),
        out_specs=P("ctx", "mem", None, None),
        check_vma=False,
    )
```

profile of v0, /device:TPU:0, one launch (start us, length us, event | category | flops | bytes accessed | tf_op | source)
XLA Modules:
  0.0 320.1 jit_solution(15708882655729172114)
XLA Ops:
  4.7 4.3 %all-to-all-start.1 = ((bf16[4,72,32]{1,2,0:T(8,128)(2,1)}), bf16[4,72,32]{1,2,0:T(8,128)(2,1)}, u32[]{:S(2)}, u32[]{:S(2)}) async-start(bf16[4,72,32]{1,2,0:T(8,128)(2,1)} %broadcast_select_fusion.3), calls=%async_computation.1 | async-start | bytes 65536 | tf_op jit(solution)/shard_map/all_to_all | solution.py:149
  9.0 2.3 gather_fusion.3
  11.3 3.7 %gather_fusion.2 = bf16[288,32,128]{2,1,0:T(8,128)(2,1)} fusion(bf16[128,32,128]{2,1,0:T(8,128)(2,1)} %bitcast.123, s32[1024]{0:T(1024)S(1)} %pad_clamp_fusion.2), kind=kCustom, calls=%fused_computation.2 | custom fusion | bytes 4719744 | tf_op jit(solution)/shard_map/gather | solution.py:137
  15.0 3.0 gather_fusion
  18.0 4.1 %broadcast_select_fusion = (bf16[4,72,32,128]{3,2,1,0:T(8,128)(2,1)S(1)}, bf16[4,72,32,128]{3,2,1,0:T(8,128)(2,1)}, bf16[4,72,32,128]{3,2,1,0:T(8,128)(2,1)}) fusion(bf16[4,72,32,128]{3,2,1,0:T(8,128)(2,1)S(1)} %bitcast.117, pred[4,72]{1,0:T(4,128)(4,1)S(1)} %bitcast.141, bf16[4,72,32,128]{3,2,1,0:T(8,128)(2,1)} %bitcast.118, ...), kind=kLoop, calls=%fused_computation.45 | loop fusion | flops 3538944 | bytes 14156064 | tf_op jit(solution)/shard_map/jit(_where)/select_n | solution.py:137
  22.1 2.4 copy.91
  24.4 3.9 %all-to-all-start.3 = ((bf16[4,72,32,128]{3,1,2,0:T(8,128)(2,1)}), bf16[4,72,32,128]{3,1,2,0:T(8,128)(2,1)S(1)}, u32[]{:S(2)}, u32[]{:S(2)}) async-start(bf16[4,72,32,128]{3,1,2,0:T(8,128)(2,1)} %copy.91), calls=%async_computation.3 | async-start | bytes 4718592 | tf_op jit(solution)/shard_map/all_to_all | solution.py:147
  28.3 4.0 %copy.82 = bf16[4,72,32,128]{3,1,2,0:T(8,128)(2,1)} copy(bf16[4,72,32,128]{3,2,1,0:T(8,128)(2,1)} %get-tuple-element.207) | data formatting | bytes 4718592 | tf_op jit(solution)/shard_map/jit(_where)/select_n | solution.py:137
  32.3 24.5 %all-to-all-done.3 = bf16[4,72,32,128]{3,1,2,0:T(8,128)(2,1)S(1)} async-done(((bf16[4,72,32,128]{3,1,2,0:T(8,128)(2,1)}), bf16[4,72,32,128]{3,1,2,0:T(8,128)(2,1)S(1)}, u32[]{:S(2)}, u32[]{:S(2)}) %all-to-all-start.3) | async-done | bytes 2359328 | tf_op jit(solution)/shard_map/all_to_all | solution.py:147
  56.8 4.5 %all-to-all-start = ((bf16[4,72,32,128]{3,1,2,0:T(8,128)(2,1)}), bf16[4,72,32,128]{3,1,2,0:T(8,128)(2,1)}, u32[]{:S(2)}, u32[]{:S(2)}) async-start(bf16[4,72,32,128]{3,1,2,0:T(8,128)(2,1)} %copy.82), calls=%async_computation | async-start | bytes 4718592 | tf_op jit(solution)/shard_map/all_to_all | solution.py:148
  68.4 4.5 %fusion.20 = (bf16[288,32,128]{2,1,0:T(8,128)(2,1)}, bf16[288,32,128]{2,1,0:T(8,128)(2,1)S(1)}) fusion(f32[288,32]{1,0:T(8,128)S(1)} %copy.93, bf16[4,72,32,128]{3,2,1,0:T(8,128)(2,1)} %copy.92), kind=kLoop, calls=%fused_computation.36 | loop fusion | flops 7077888 | bytes 7114752 | tf_op jit(solution)/shard_map/convert_element_type | solution.py:17
  72.8 17.0 %all-to-all-done = bf16[4,72,32,128]{3,1,2,0:T(8,128)(2,1)} async-done(((bf16[4,72,32,128]{3,1,2,0:T(8,128)(2,1)}), bf16[4,72,32,128]{3,1,2,0:T(8,128)(2,1)}, u32[]{:S(2)}, u32[]{:S(2)}) %all-to-all-start) | async-done | bytes 2359328 | tf_op jit(solution)/shard_map/all_to_all | solution.py:148
  89.9 6.6 %all-to-all-start.5 = ((bf16[8,2,256]{2,1,0:T(2,128)(2,1)}), bf16[8,2,256]{2,1,0:T(2,128)(2,1)S(1)}, u32[]{:S(2)}, u32[]{:S(2)}) async-start(bf16[8,2,256]{2,1,0:T(2,128)(2,1)} %reshape.334), calls=%async_computation.5 | async-start | bytes 16384 | tf_op jit(solution)/shard_map/all_to_all | solution.py:59
  96.5 1.9 copy.83
  98.3 2.2 fusion.21
  100.8 2.3 add_convert_fusion
  103.2 16.7 %copy.131 = bf16[1,4096,128]{2,0,1:T(2,128)(2,1)S(1)} copy(bf16[1,4096,128]{2,1,0:T(8,128)(2,1)S(1)} %bitcast.125) | data formatting | bytes 2097152 | tf_op jit(solution)/shard_map/convert_element_type | solution.py:53
  119.9 22.4 %reduce.12 = bf16[4096,128]{1,0:T(8,128)(2,1)S(1)} reduce(bf16[4096,1,128]{2,1,0:T(2,128)(2,1)S(1)} %bitcast.122, bf16[]{:T(256)} %broadcast.245), dimensions={1}, to_apply=%bitcast.100.reduce_sub_computation | reduce | bytes 2097154
  143.4 6.0 %all-to-all-start.4 = ((bf16[8,2,32768]{2,1,0:T(2,128)(2,1)}), bf16[8,2,32768]{2,1,0:T(2,128)(2,1)S(1)}, u32[]{:S(2)}, u32[]{:S(2)}) async-start(bf16[8,2,32768]{2,1,0:T(2,128)(2,1)} %reshape.332), calls=%async_computation.4 | async-start | bytes 2097152 | tf_op jit(solution)/shard_map/all_to_all | solution.py:52
  149.4 2.4 copy.89
  152.0 22.6 %all-to-all-done.4 = bf16[8,2,32768]{2,1,0:T(2,128)(2,1)S(1)} async-done(((bf16[8,2,32768]{2,1,0:T(2,128)(2,1)}), bf16[8,2,32768]{2,1,0:T(2,128)(2,1)S(1)}, u32[]{:S(2)}, u32[]{:S(2)}) %all-to-all-start.4) | async-done | bytes 1048608 | tf_op jit(solution)/shard_map/all_to_all | solution.py:52
  174.6 4.7 %all-to-all-start.2 = ((bf16[4,72,32,128]{3,1,2,0:T(8,128)(2,1)}), bf16[4,72,32,128]{3,1,2,0:T(8,128)(2,1)}, u32[]{:S(2)}, u32[]{:S(2)}) async-start(bf16[4,72,32,128]{3,1,2,0:T(8,128)(2,1)} %copy.89), calls=%async_computation.2 | async-start | bytes 4718592 | tf_op jit(solution)/shard_map/all_to_all | solution.py:146
  179.3 3.5 %reshape.333 = bf16[4096,1,128]{2,1,0:T(2,128)(2,1)} reshape(bf16[8,2,32768]{2,1,0:T(2,128)(2,1)S(1)} %all-to-all-done.4) | data formatting | bytes 2097152
  182.7 3.8 %bitcast_convert_fusion.1 = f32[1,4096,128]{2,0,1:T(1,128)S(1)} fusion(bf16[4096,1,128]{2,1,0:T(2,128)(2,1)} %reshape.333), kind=kLoop, calls=%fused_computation.114 | loop fusion | flops 524288 | bytes 3145728 | tf_op jit(solution)/shard_map/convert_element_type | solution.py:58
  186.5 1.9 slice.138
  193.6 2.7 pad.29
  196.3 2.4 add.166
  199.7 2.8 pad.43
  205.5 2.1 all-to-all-done.2
  207.6 3.6 %all-to-all-start.6 = ((bf16[8,512,128]{2,1,0:T(8,128)(2,1)}), bf16[8,512,128]{2,1,0:T(8,128)(2,1)S(1)}, u32[]{:S(2)}, u32[]{:S(2)}) async-start(bf16[8,512,128]{2,1,0:T(8,128)(2,1)} %concatenate.11), calls=%async_computation.6 | async-start | bytes 2097152 | tf_op jit(solution)/shard_map/all_to_all | solution.py:69
  211.2 3.6 %copy.90 = bf16[4,72,32,128]{3,2,1,0:T(8,128)(2,1)} copy(bf16[4,72,32,128]{3,1,2,0:T(8,128)(2,1)} %all-to-all-done.2) | data formatting | bytes 4718592 | tf_op jit(solution)/shard_map/all_to_all | solution.py:146
  214.7 22.1 %all-to-all-done.6 = bf16[8,512,128]{2,1,0:T(8,128)(2,1)S(1)} async-done(((bf16[8,512,128]{2,1,0:T(8,128)(2,1)}), bf16[8,512,128]{2,1,0:T(8,128)(2,1)S(1)}, u32[]{:S(2)}, u32[]{:S(2)}) %all-to-all-start.6) | async-done | bytes 1048608 | tf_op jit(solution)/shard_map/all_to_all | solution.py:69
  240.2 33.5 %while.14 = (s32[]{:T(128)}, bf16[288,32,128]{2,0,1:T(8,128)(2,1)}, bf16[288,32,128]{2,0,1:T(8,128)(2,1)}, f32[288,32]{0,1:T(8,128)}, bf16[288,32,128]{2,1,0:T(8...) while((s32[]{:T(128)}, bf16[288,32,128]{2,0,1:T(8,128)(2,1)}, ...), condition=%wide.region_7.8_spmd.clone, body=%wide.region_6.7_spmd.clone.sunk | while | flops 495840512 | bytes 11659435 | solution.py:109
  242.3 2.6 convolution_bitcast_fusion.2
  246.2 2.3 fusion.66
  250.6 2.6 convolution_bitcast_fusion.2
  254.5 2.3 fusion.66
  258.9 2.6 convolution_bitcast_fusion.2
  262.8 2.4 fusion.66
  267.3 2.6 convolution_bitcast_fusion.2
  271.3 2.4 fusion.66
  273.7 4.0 %copy.102 = bf16[4,72,32,128]{3,2,1,0:T(8,128)(2,1)} copy(bf16[4,72,32,128]{3,1,0,2:T(8,128)(2,1)} %bitcast.116) | data formatting | bytes 4718592 | tf_op jit(solution)/shard_map/reshape | solution.py:166
  277.7 3.8 %all-to-all-start.7 = ((bf16[4,72,32,128]{3,2,1,0:T(8,128)(2,1)}), bf16[4,72,32,128]{3,2,1,0:T(8,128)(2,1)S(1)}, u32[]{:S(2)}, u32[]{:S(2)}) async-start(bf16[4,72,32,128]{3,2,1,0:T(8,128)(2,1)} %copy.102), calls=%async_computation.7 | async-start | bytes 4718592 | tf_op jit(solution)/shard_map/all_to_all | solution.py:165
  281.7 1.9 gather_fusion.6
  284.1 25.8 %all-to-all-done.7 = bf16[4,72,32,128]{3,2,1,0:T(8,128)(2,1)S(1)} async-done(((bf16[4,72,32,128]{3,2,1,0:T(8,128)(2,1)}), bf16[4,72,32,128]{3,2,1,0:T(8,128)(2,1)S(1)}, u32[]{:S(2)}, u32[]{:S(2)}) %all-to-all-start.7) | async-done | bytes 2359328 | tf_op jit(solution)/shard_map/all_to_all | solution.py:165
  311.3 2.4 gather_fusion.5
  313.7 2.4 gather_fusion.4
  317.5 2.7 fusion.29
  (120 shorter events, 42.7 us)
Async XLA Ops:
  0.0 9.0 %copy-start = (bf16[1,128,32,128]{3,2,1,0:T(8,128)(2,1)S(1)}, bf16[1,128,32,128]{3,2,1,0:T(8,128)(2,1)}, u32[]{:S(2)}) copy-start(bf16[1,128,32,128]{3,2,1,0:T(8,128)(2,1)} %param.10) | copy-start | bytes 3145732
  4.7 19.7 %all-to-all-start.1 = ((bf16[4,72,32]{1,2,0:T(8,128)(2,1)}), bf16[4,72,32]{1,2,0:T(8,128)(2,1)}, u32[]{:S(2)}, u32[]{:S(2)}) async-start(bf16[4,72,32]{1,2,0:T(8,128)(2,1)} %broadcast_select_fusion.3), calls=%async_computation.1 | async-start | bytes 65536 | tf_op jit(solution)/shard_map/all_to_all | solution.py:149
  11.3 3.7 %copy-start.7 = (bf16[1,128,32,128]{3,2,1,0:T(8,128)(2,1)S(1)}, bf16[1,128,32,128]{3,2,1,0:T(8,128)(2,1)}, u32[]{:S(2)}) copy-start(bf16[1,128,32,128]{3,2,1,0:T(8,128)(2,1)} %param.11) | copy-start | bytes 3145732
  24.4 32.4 %all-to-all-start.3 = ((bf16[4,72,32,128]{3,1,2,0:T(8,128)(2,1)}), bf16[4,72,32,128]{3,1,2,0:T(8,128)(2,1)S(1)}, u32[]{:S(2)}, u32[]{:S(2)}) async-start(bf16[4,72,32,128]{3,1,2,0:T(8,128)(2,1)} %copy.91), calls=%async_computation.3 | async-start | bytes 4718592 | tf_op jit(solution)/shard_map/all_to_all | solution.py:147
  56.8 33.0 %all-to-all-start = ((bf16[4,72,32,128]{3,1,2,0:T(8,128)(2,1)}), bf16[4,72,32,128]{3,1,2,0:T(8,128)(2,1)}, u32[]{:S(2)}, u32[]{:S(2)}) async-start(bf16[4,72,32,128]{3,1,2,0:T(8,128)(2,1)} %copy.82), calls=%async_computation | async-start | bytes 4718592 | tf_op jit(solution)/shard_map/all_to_all | solution.py:148
  89.9 53.6 %all-to-all-start.5 = ((bf16[8,2,256]{2,1,0:T(2,128)(2,1)}), bf16[8,2,256]{2,1,0:T(2,128)(2,1)S(1)}, u32[]{:S(2)}, u32[]{:S(2)}) async-start(bf16[8,2,256]{2,1,0:T(2,128)(2,1)} %reshape.334), calls=%async_computation.5 | async-start | bytes 16384 | tf_op jit(solution)/shard_map/all_to_all | solution.py:59
  98.3 2.2 copy-start.2
  98.3 2.5 copy-start.3
  142.3 7.1 %copy-start.4 = (bf16[4,72,32,128]{3,2,1,0:T(8,128)(2,1)S(1)}, bf16[4,72,32,128]{3,2,1,0:T(8,128)(2,1)}, u32[]{:S(2)}) copy-start(bf16[4,72,32,128]{3,2,1,0:T(8,128)(2,1)} %get-tuple-element.206) | copy-start | bytes 7077892
  143.4 31.1 %all-to-all-start.4 = ((bf16[8,2,32768]{2,1,0:T(2,128)(2,1)}), bf16[8,2,32768]{2,1,0:T(2,128)(2,1)S(1)}, u32[]{:S(2)}, u32[]{:S(2)}) async-start(bf16[8,2,32768]{2,1,0:T(2,128)(2,1)} %reshape.332), calls=%async_computation.4 | async-start | bytes 2097152 | tf_op jit(solution)/shard_map/all_to_all | solution.py:52
  174.6 33.0 %all-to-all-start.2 = ((bf16[4,72,32,128]{3,1,2,0:T(8,128)(2,1)}), bf16[4,72,32,128]{3,1,2,0:T(8,128)(2,1)}, u32[]{:S(2)}, u32[]{:S(2)}) async-start(bf16[4,72,32,128]{3,1,2,0:T(8,128)(2,1)} %copy.89), calls=%async_computation.2 | async-start | bytes 4718592 | tf_op jit(solution)/shard_map/all_to_all | solution.py:146
  189.1 0.7 copy-start.9
  196.3 2.4 copy-start.6
  198.7 1.0 copy-start.10
  199.6 2.9 copy-start.8
  207.6 29.2 %all-to-all-start.6 = ((bf16[8,512,128]{2,1,0:T(8,128)(2,1)}), bf16[8,512,128]{2,1,0:T(8,128)(2,1)S(1)}, u32[]{:S(2)}, u32[]{:S(2)}) async-start(bf16[8,512,128]{2,1,0:T(8,128)(2,1)} %concatenate.11), calls=%async_computation.6 | async-start | bytes 2097152 | tf_op jit(solution)/shard_map/all_to_all | solution.py:69
  277.7 3.8 %copy-start.12 = (s32[1,128,2]{1,2,0:T(2,128)S(1)}, s32[1,128,2]{1,2,0:T(2,128)}, u32[]{:S(2)}) copy-start(s32[1,128,2]{1,2,0:T(2,128)} %param.13) | copy-start | bytes 3076
  277.7 32.2 %all-to-all-start.7 = ((bf16[4,72,32,128]{3,2,1,0:T(8,128)(2,1)}), bf16[4,72,32,128]{3,2,1,0:T(8,128)(2,1)S(1)}, u32[]{:S(2)}, u32[]{:S(2)}) async-start(bf16[4,72,32,128]{3,2,1,0:T(8,128)(2,1)} %copy.102), calls=%async_computation.7 | async-start | bytes 4718592 | tf_op jit(solution)/shard_map/all_to_all | solution.py:165
  281.7 2.3 copy-start.13
  309.9 1.4 copy-start.5
  313.7 3.7 %copy-start.11 = (f32[4096]{0:T(1024)S(1)}, f32[4096]{0:T(1024)}, u32[]{:S(2)}) copy-start(f32[4096]{0:T(1024)} %param.15) | copy-start | bytes 49156
  316.2 4.0 %copy-start.1 = (bf16[1,128,32,128]{3,2,1,0:T(8,128)(2,1)S(1)}, bf16[1,128,32,128]{3,2,1,0:T(8,128)(2,1)}, u32[]{:S(2)}) copy-start(bf16[1,128,32,128]{3,2,1,0:T(8,128)(2,1)} %param.10) | copy-start | bytes 3145732
where the time goes:
time: 322 us; the launch traced here: 320 us
  waiting for transfers between devices  114 us (35%)
  local copies, waits for them, and re-layouts  83.6 us (26%)
  other arithmetic  55 us (17%)
  starting transfers between devices  37.3 us (12%)
  matrix products  29.6 us (9%)
    all_to_all x1, waiting for transfers between devices, shards(): lax.all_to_all(readout.reshape(memories, capacity, heads, hdim), 'mem', s...  25.8 us
    all_to_all x1, waiting for transfers between devices, shards(): lax.all_to_all(key_send, 'mem', split_axis=0, concat_axis=0, tiled=True)  24.5 us
    unnamed x2, other arithmetic  23.1 us
    all_to_all x1, waiting for transfers between devices, incoming_state(): lax.all_to_all(state_increment.reshape(1, flat_rows, hdim).astype(jnp.bfl...  22.6 us
    all_to_all x1, waiting for transfers between devices, incoming_state(): lax.all_to_all(as_sent(shifted), 'ctx', split_axis=0, concat_axis=1, tile...  22.1 us
    all_to_all x1, waiting for transfers between devices, shards(): lax.all_to_all(value_send, 'mem', split_axis=0, concat_axis=0, tiled=True)  17 us
    convert_element_type x1, local copies, waits for them, and re-layouts, incoming_state(): state_increment.reshape(1, flat_rows, hdim).astype(jnp.bfloat16)  16.7 us
    unnamed x37, local copies, waits for them, and re-layouts  10.6 us
  transfers between devices with their start and end apart: 8, of which 6 were waited for; matrix products, arithmetic and copies ran while one was open for 35% of the time, Pallas kernels for 0%

commit v1 on v0

--- a/solution.py
+++ b/solution.py
@@ -49,12 +49,20 @@
     hdim = state_increment.shape[1]
     flat_rows = heads * hdim
     pieces = (
-        lax.all_to_all(
-            state_increment.reshape(1, flat_rows, hdim).astype(jnp.bfloat16),
-            "ctx",
-            split_axis=1,
-            concat_axis=0,
-            tiled=True,
+        jnp.concatenate(
+            lax.all_to_all(
+                jnp.stack(
+                    jnp.split(
+                        state_increment.reshape(1, flat_rows, hdim).astype(jnp.bfloat16),
+                        lax.axis_size("ctx"),
+                        axis=1,
+                    )
+                ),
+                "ctx",
+                0,
+                0,
+            ),
+            axis=0,
         ).astype(jnp.float32),
         lax.all_to_all(
             jnp.repeat(decay_total, hdim).reshape(1, flat_rows).astype(jnp.bfloat16),

time: 322 us -> 287 us (0.89)
  other arithmetic: 55 us -> 30.5 us
  local copies, waits for them, and re-layouts: 83.6 us -> 66 us
  waiting for transfers between devices: 114 us -> 122 us
    unnamed x2 -> x1, other arithmetic: 23.1 us -> 0.69 us
    convert_element_type x1 -> x0, local copies, waits for them, and re-layouts: 16.7 us -> none  [incoming_state(): state_increment.reshape(1, flat_rows, hdim).astype(jnp.bfloat16)]
    all_to_all x1, waiting for transfers between devices: 2.13 us -> 9.47 us  [shards(): lax.all_to_all(query_send, 'mem', split_axis=0, concat_axis=0, tiled=True)]
    unnamed x37 -> x40, local copies, waits for them, and re-layouts: 10.6 us -> 9.98 us
  transfers between devices with their start and end apart: 8 -> 8, of which waited for: 6 -> 6; matrix products, arithmetic and copies ran while one was open for 35% -> 24% of each run, Pallas kernels for 0% -> 0%
where the time goes in v1:
time: 287 us; the launch traced here: 285 us
  waiting for transfers between devices  122 us (43%)
  local copies, waits for them, and re-layouts  66 us (23%)
  starting transfers between devices  37 us (13%)
  other arithmetic  30.5 us (11%)
  matrix products  29.6 us (10%)
    all_to_all x1, waiting for transfers between devices, shards(): lax.all_to_all(readout.reshape(memories, capacity, heads, hdim), 'mem', s...  25.8 us
    all_to_all x1, waiting for transfers between devices, shards(): lax.all_to_all(key_send, 'mem', split_axis=0, concat_axis=0, tiled=True)  24.5 us
    all_to_all x1, waiting for transfers between devices, incoming_state(): lax.all_to_all(jnp.stack(jnp.split(state_increment.reshape(1, flat_rows,...  22.6 us
    all_to_all x1, waiting for transfers between devices, incoming_state(): lax.all_to_all(as_sent(shifted), 'ctx', split_axis=0, concat_axis=1, tile...  22.1 us
    all_to_all x1, waiting for transfers between devices, shards(): lax.all_to_all(value_send, 'mem', split_axis=0, concat_axis=0, tiled=True)  17 us
    gather x5, local copies, waits for them, and re-layouts, packed(): rows_out = jnp.where(shaped, table[source], jnp.zeros((), table.dtype))  10.4 us
    dot_general x4, matrix products, one_group(): jnp.einsum('hij,jhd->ihd', weights, group_value, preferred_element_type=j...  10.3 us
    unnamed x40, local copies, waits for them, and re-layouts  9.98 us
  transfers between devices with their start and end apart: 8, of which 6 were waited for; matrix products, arithmetic and copies ran while one was open for 24% of the time, Pallas kernels for 0%

profile of v1, /device:TPU:0, one launch (start us, length us, event | category | flops | bytes accessed | tf_op | source)
XLA Modules:
  0.0 285.2 jit_solution(17300565901519007638)
XLA Ops:
  4.7 4.3 %all-to-all-start.1 = ((bf16[4,72,32]{1,2,0:T(8,128)(2,1)}), bf16[4,72,32]{1,2,0:T(8,128)(2,1)}, u32[]{:S(2)}, u32[]{:S(2)}) async-start(bf16[4,72,32]{1,2,0:T(8,128)(2,1)} %broadcast_select_fusion.3), calls=%async_computation.1 | async-start | bytes 65536 | tf_op jit(solution)/shard_map/all_to_all | solution.py:157
  9.0 2.3 gather_fusion.3
  11.3 3.7 %gather_fusion.2 = bf16[288,32,128]{2,1,0:T(8,128)(2,1)} fusion(bf16[128,32,128]{2,1,0:T(8,128)(2,1)} %bitcast.148, s32[1024]{0:T(1024)S(1)} %pad_clamp_fusion.2), kind=kCustom, calls=%fused_computation.2 | custom fusion | bytes 4719744 | tf_op jit(solution)/shard_map/gather | solution.py:145
  15.0 3.0 %gather_fusion = bf16[288,32,128]{2,1,0:T(8,128)(2,1)} fusion(bf16[128,32,128]{2,1,0:T(8,128)(2,1)S(1)} %bitcast.149, s32[1024]{0:T(1024)S(1)} %pad_clamp_fusion.2), kind=kCustom, calls=%fused_computation | custom fusion | bytes 4719744 | tf_op jit(solution)/shard_map/gather | solution.py:145
  18.0 4.1 %broadcast_select_fusion = (bf16[4,72,32,128]{3,2,1,0:T(8,128)(2,1)S(1)}, bf16[4,72,32,128]{3,2,1,0:T(8,128)(2,1)}, bf16[4,72,32,128]{3,2,1,0:T(8,128)(2,1)}) fusion(bf16[4,72,32,128]{3,2,1,0:T(8,128)(2,1)S(1)} %bitcast.143, pred[4,72]{1,0:T(4,128)(4,1)S(1)} %bitcast.172, bf16[4,72,32,128]{3,2,1,0:T(8,128)(2,1)} %bitcast.144, ...), kind=kLoop, calls=%fused_computation.45 | loop fusion | flops 3538944 | bytes 14156064 | tf_op jit(solution)/shard_map/jit(_where)/select_n | solution.py:145
  22.1 2.4 copy.87
  24.4 3.9 %all-to-all-start.3 = ((bf16[4,72,32,128]{3,1,2,0:T(8,128)(2,1)}), bf16[4,72,32,128]{3,1,2,0:T(8,128)(2,1)S(1)}, u32[]{:S(2)}, u32[]{:S(2)}) async-start(bf16[4,72,32,128]{3,1,2,0:T(8,128)(2,1)} %copy.87), calls=%async_computation.3 | async-start | bytes 4718592 | tf_op jit(solution)/shard_map/all_to_all | solution.py:155
  28.3 4.0 %copy.78 = bf16[4,72,32,128]{3,1,2,0:T(8,128)(2,1)} copy(bf16[4,72,32,128]{3,2,1,0:T(8,128)(2,1)} %get-tuple-element.209) | data formatting | bytes 4718592 | tf_op jit(solution)/shard_map/jit(_where)/select_n | solution.py:145
  32.3 24.5 %all-to-all-done.3 = bf16[4,72,32,128]{3,1,2,0:T(8,128)(2,1)S(1)} async-done(((bf16[4,72,32,128]{3,1,2,0:T(8,128)(2,1)}), bf16[4,72,32,128]{3,1,2,0:T(8,128)(2,1)S(1)}, u32[]{:S(2)}, u32[]{:S(2)}) %all-to-all-start.3) | async-done | bytes 2359328 | tf_op jit(solution)/shard_map/all_to_all | solution.py:155
  56.8 4.5 %all-to-all-start = ((bf16[4,72,32,128]{3,1,2,0:T(8,128)(2,1)}), bf16[4,72,32,128]{3,1,2,0:T(8,128)(2,1)}, u32[]{:S(2)}, u32[]{:S(2)}) async-start(bf16[4,72,32,128]{3,1,2,0:T(8,128)(2,1)} %copy.78), calls=%async_computation | async-start | bytes 4718592 | tf_op jit(solution)/shard_map/all_to_all | solution.py:156
  66.6 1.8 copy.88
  68.4 4.5 %fusion.20 = (bf16[288,32,128]{2,1,0:T(8,128)(2,1)}, bf16[288,32,128]{2,1,0:T(8,128)(2,1)S(1)}) fusion(f32[288,32]{1,0:T(8,128)S(1)} %copy.89, bf16[4,72,32,128]{3,2,1,0:T(8,128)(2,1)} %copy.88), kind=kLoop, calls=%fused_computation.36 | loop fusion | flops 7077888 | bytes 7114752 | tf_op jit(solution)/shard_map/convert_element_type | solution.py:17
  72.8 17.0 %all-to-all-done = bf16[4,72,32,128]{3,1,2,0:T(8,128)(2,1)} async-done(((bf16[4,72,32,128]{3,1,2,0:T(8,128)(2,1)}), bf16[4,72,32,128]{3,1,2,0:T(8,128)(2,1)}, u32[]{:S(2)}, u32[]{:S(2)}) %all-to-all-start) | async-done | bytes 2359328 | tf_op jit(solution)/shard_map/all_to_all | solution.py:156
  89.9 6.6 %all-to-all-start.5 = ((bf16[8,2,256]{2,1,0:T(2,128)(2,1)}), bf16[8,2,256]{2,1,0:T(2,128)(2,1)S(1)}, u32[]{:S(2)}, u32[]{:S(2)}) async-start(bf16[8,2,256]{2,1,0:T(2,128)(2,1)} %reshape.330), calls=%async_computation.5 | async-start | bytes 16384 | tf_op jit(solution)/shard_map/all_to_all | solution.py:67
  96.5 1.9 copy.79
  98.3 2.2 fusion.21
  100.8 2.3 add_convert_fusion
  108.5 6.0 %all-to-all-start.4 = ((bf16[8,1,512,128]{3,2,1,0:T(8,128)(2,1)}), bf16[8,1,512,128]{3,2,1,0:T(8,128)(2,1)S(1)}, u32[]{:S(2)}, u32[]{:S(2)}) async-start(bf16[8,1,512,128]{3,2,1,0:T(8,128)(2,1)} %fusion.42), calls=%async_computation.4 | async-start | bytes 2097152 | tf_op jit(solution)/shard_map/all_to_all | solution.py:53
  114.5 2.4 copy.85
  117.0 22.6 %all-to-all-done.4 = bf16[8,1,512,128]{3,2,1,0:T(8,128)(2,1)S(1)} async-done(((bf16[8,1,512,128]{3,2,1,0:T(8,128)(2,1)}), bf16[8,1,512,128]{3,2,1,0:T(8,128)(2,1)S(1)}, u32[]{:S(2)}, u32[]{:S(2)}) %all-to-all-start.4) | async-done | bytes 1048608 | tf_op jit(solution)/shard_map/all_to_all | solution.py:53
  139.6 4.5 %all-to-all-start.2 = ((bf16[4,72,32,128]{3,1,2,0:T(8,128)(2,1)}), bf16[4,72,32,128]{3,1,2,0:T(8,128)(2,1)}, u32[]{:S(2)}, u32[]{:S(2)}) async-start(bf16[4,72,32,128]{3,1,2,0:T(8,128)(2,1)} %copy.85), calls=%async_computation.2 | async-start | bytes 4718592 | tf_op jit(solution)/shard_map/all_to_all | solution.py:154
  144.1 1.7 fusion.58
  149.2 1.8 pad_add_fusion
  151.0 2.7 pad.29
  153.7 2.4 add.166
  157.4 2.8 pad.43
  160.4 1.7 add_convert_fusion.1
  163.2 9.5 %all-to-all-done.2 = bf16[4,72,32,128]{3,1,2,0:T(8,128)(2,1)} async-done(((bf16[4,72,32,128]{3,1,2,0:T(8,128)(2,1)}), bf16[4,72,32,128]{3,1,2,0:T(8,128)(2,1)}, u32[]{:S(2)}, u32[]{:S(2)}) %all-to-all-start.2) | async-done | bytes 2359328 | tf_op jit(solution)/shard_map/all_to_all | solution.py:154
  172.7 3.6 %all-to-all-start.6 = ((bf16[8,512,128]{2,1,0:T(8,128)(2,1)}), bf16[8,512,128]{2,1,0:T(8,128)(2,1)S(1)}, u32[]{:S(2)}, u32[]{:S(2)}) async-start(bf16[8,512,128]{2,1,0:T(8,128)(2,1)} %concatenate.11), calls=%async_computation.6 | async-start | bytes 2097152 | tf_op jit(solution)/shard_map/all_to_all | solution.py:77
  176.2 3.6 %copy.86 = bf16[4,72,32,128]{3,2,1,0:T(8,128)(2,1)} copy(bf16[4,72,32,128]{3,1,2,0:T(8,128)(2,1)} %all-to-all-done.2) | data formatting | bytes 4718592 | tf_op jit(solution)/shard_map/all_to_all | solution.py:154
  179.8 22.1 %all-to-all-done.6 = bf16[8,512,128]{2,1,0:T(8,128)(2,1)S(1)} async-done(((bf16[8,512,128]{2,1,0:T(8,128)(2,1)}), bf16[8,512,128]{2,1,0:T(8,128)(2,1)S(1)}, u32[]{:S(2)}, u32[]{:S(2)}) %all-to-all-start.6) | async-done | bytes 1048608 | tf_op jit(solution)/shard_map/all_to_all | solution.py:77
  203.4 1.8 broadcast_in_dim.102
  205.2 33.5 %while.14 = (s32[]{:T(128)}, bf16[288,32,128]{2,0,1:T(8,128)(2,1)}, bf16[288,32,128]{2,0,1:T(8,128)(2,1)}, f32[288,32]{0,1:T(8,128)}, bf16[288,32,128]{2,1,0:T(8...) while((s32[]{:T(128)}, bf16[288,32,128]{2,0,1:T(8,128)(2,1)}, ...), condition=%wide.region_7.8_spmd.clone, body=%wide.region_6.7_spmd.clone.sunk | while | flops 495840512 | bytes 11659435 | solution.py:117
  207.3 2.6 convolution_bitcast_fusion.2
  211.2 2.3 fusion.75
  215.7 2.6 convolution_bitcast_fusion.2
  219.6 2.3 fusion.75
  224.0 2.6 convolution_bitcast_fusion.2
  227.9 2.4 fusion.75
  232.4 2.6 convolution_bitcast_fusion.2
  236.3 2.4 fusion.75
  238.7 4.0 %copy.96 = bf16[4,72,32,128]{3,2,1,0:T(8,128)(2,1)} copy(bf16[4,72,32,128]{3,1,0,2:T(8,128)(2,1)} %bitcast.142) | data formatting | bytes 4718592 | tf_op jit(solution)/shard_map/reshape | solution.py:174
  242.7 3.8 %all-to-all-start.7 = ((bf16[4,72,32,128]{3,2,1,0:T(8,128)(2,1)}), bf16[4,72,32,128]{3,2,1,0:T(8,128)(2,1)S(1)}, u32[]{:S(2)}, u32[]{:S(2)}) async-start(bf16[4,72,32,128]{3,2,1,0:T(8,128)(2,1)} %copy.96), calls=%async_computation.7 | async-start | bytes 4718592 | tf_op jit(solution)/shard_map/all_to_all | solution.py:173
  246.8 1.9 gather_fusion.6
  249.1 25.8 %all-to-all-done.7 = bf16[4,72,32,128]{3,2,1,0:T(8,128)(2,1)S(1)} async-done(((bf16[4,72,32,128]{3,2,1,0:T(8,128)(2,1)}), bf16[4,72,32,128]{3,2,1,0:T(8,128)(2,1)S(1)}, u32[]{:S(2)}, u32[]{:S(2)}) %all-to-all-start.7) | async-done | bytes 2359328 | tf_op jit(solution)/shard_map/all_to_all | solution.py:173
  276.4 2.4 gather_fusion.5
  278.8 2.4 gather_fusion.4
  282.5 2.7 fusion.29
  (122 shorter events, 40.2 us)
Async XLA Ops:
  0.0 9.0 %copy-start = (bf16[1,128,32,128]{3,2,1,0:T(8,128)(2,1)S(1)}, bf16[1,128,32,128]{3,2,1,0:T(8,128)(2,1)}, u32[]{:S(2)}) copy-start(bf16[1,128,32,128]{3,2,1,0:T(8,128)(2,1)} %param.10) | copy-start | bytes 3145732
  4.7 19.7 %all-to-all-start.1 = ((bf16[4,72,32]{1,2,0:T(8,128)(2,1)}), bf16[4,72,32]{1,2,0:T(8,128)(2,1)}, u32[]{:S(2)}, u32[]{:S(2)}) async-start(bf16[4,72,32]{1,2,0:T(8,128)(2,1)} %broadcast_select_fusion.3), calls=%async_computation.1 | async-start | bytes 65536 | tf_op jit(solution)/shard_map/all_to_all | solution.py:157
  11.3 3.7 %copy-start.7 = (bf16[1,128,32,128]{3,2,1,0:T(8,128)(2,1)S(1)}, bf16[1,128,32,128]{3,2,1,0:T(8,128)(2,1)}, u32[]{:S(2)}) copy-start(bf16[1,128,32,128]{3,2,1,0:T(8,128)(2,1)} %param.11) | copy-start | bytes 3145732
  24.4 32.4 %all-to-all-start.3 = ((bf16[4,72,32,128]{3,1,2,0:T(8,128)(2,1)}), bf16[4,72,32,128]{3,1,2,0:T(8,128)(2,1)S(1)}, u32[]{:S(2)}, u32[]{:S(2)}) async-start(bf16[4,72,32,128]{3,1,2,0:T(8,128)(2,1)} %copy.87), calls=%async_computation.3 | async-start | bytes 4718592 | tf_op jit(solution)/shard_map/all_to_all | solution.py:155
  56.8 33.0 %all-to-all-start = ((bf16[4,72,32,128]{3,1,2,0:T(8,128)(2,1)}), bf16[4,72,32,128]{3,1,2,0:T(8,128)(2,1)}, u32[]{:S(2)}, u32[]{:S(2)}) async-start(bf16[4,72,32,128]{3,1,2,0:T(8,128)(2,1)} %copy.78), calls=%async_computation | async-start | bytes 4718592 | tf_op jit(solution)/shard_map/all_to_all | solution.py:156
  89.9 18.6 %all-to-all-start.5 = ((bf16[8,2,256]{2,1,0:T(2,128)(2,1)}), bf16[8,2,256]{2,1,0:T(2,128)(2,1)S(1)}, u32[]{:S(2)}, u32[]{:S(2)}) async-start(bf16[8,2,256]{2,1,0:T(2,128)(2,1)} %reshape.330), calls=%async_computation.5 | async-start | bytes 16384 | tf_op jit(solution)/shard_map/all_to_all | solution.py:67
  98.3 2.2 copy-start.2
  98.3 2.5 copy-start.3
  103.2 11.3 %copy-start.4 = (bf16[4,72,32,128]{3,2,1,0:T(8,128)(2,1)S(1)}, bf16[4,72,32,128]{3,2,1,0:T(8,128)(2,1)}, u32[]{:S(2)}) copy-start(bf16[4,72,32,128]{3,2,1,0:T(8,128)(2,1)} %get-tuple-element.208) | copy-start | bytes 7077892
  108.5 31.1 %all-to-all-start.4 = ((bf16[8,1,512,128]{3,2,1,0:T(8,128)(2,1)}), bf16[8,1,512,128]{3,2,1,0:T(8,128)(2,1)S(1)}, u32[]{:S(2)}, u32[]{:S(2)}) async-start(bf16[8,1,512,128]{3,2,1,0:T(8,128)(2,1)} %fusion.42), calls=%async_computation.4 | async-start | bytes 2097152 | tf_op jit(solution)/shard_map/all_to_all | solution.py:53
  139.6 33.0 %all-to-all-start.2 = ((bf16[4,72,32,128]{3,1,2,0:T(8,128)(2,1)}), bf16[4,72,32,128]{3,1,2,0:T(8,128)(2,1)}, u32[]{:S(2)}, u32[]{:S(2)}) async-start(bf16[4,72,32,128]{3,1,2,0:T(8,128)(2,1)} %copy.85), calls=%async_computation.2 | async-start | bytes 4718592 | tf_op jit(solution)/shard_map/all_to_all | solution.py:154
  146.5 0.7 copy-start.9
  153.7 3.4 %copy-start.6 = (f32[4,512,128]{2,1,0:T(8,128)S(1)}, f32[4,512,128]{2,1,0:T(8,128)}, u32[]{:S(2)}) copy-start(f32[4,512,128]{2,1,0:T(8,128)} %pad.29) | copy-start | bytes 3145732
  157.4 2.9 %copy-start.8 = (f32[4,512,128]{2,1,0:T(8,128)S(1)}, f32[4,512,128]{2,1,0:T(8,128)}, u32[]{:S(2)}) copy-start(f32[4,512,128]{2,1,0:T(8,128)} %add.166) | copy-start | bytes 3145732
  172.7 29.2 %all-to-all-start.6 = ((bf16[8,512,128]{2,1,0:T(8,128)(2,1)}), bf16[8,512,128]{2,1,0:T(8,128)(2,1)S(1)}, u32[]{:S(2)}, u32[]{:S(2)}) async-start(bf16[8,512,128]{2,1,0:T(8,128)(2,1)} %concatenate.11), calls=%async_computation.6 | async-start | bytes 2097152 | tf_op jit(solution)/shard_map/all_to_all | solution.py:77
  242.7 3.8 %copy-start.11 = (s32[1,128,2]{1,2,0:T(2,128)S(1)}, s32[1,128,2]{1,2,0:T(2,128)}, u32[]{:S(2)}) copy-start(s32[1,128,2]{1,2,0:T(2,128)} %param.13) | copy-start | bytes 3076
  242.7 32.2 %all-to-all-start.7 = ((bf16[4,72,32,128]{3,2,1,0:T(8,128)(2,1)}), bf16[4,72,32,128]{3,2,1,0:T(8,128)(2,1)S(1)}, u32[]{:S(2)}, u32[]{:S(2)}) async-start(bf16[4,72,32,128]{3,2,1,0:T(8,128)(2,1)} %copy.96), calls=%async_computation.7 | async-start | bytes 4718592 | tf_op jit(solution)/shard_map/all_to_all | solution.py:173
  246.8 2.3 copy-start.12
  274.9 1.4 copy-start.5
  278.8 3.7 %copy-start.10 = (f32[4096]{0:T(1024)S(1)}, f32[4096]{0:T(1024)}, u32[]{:S(2)}) copy-start(f32[4096]{0:T(1024)} %param.15) | copy-start | bytes 49156
  281.2 4.0 %copy-start.1 = (bf16[1,128,32,128]{3,2,1,0:T(8,128)(2,1)S(1)}, bf16[1,128,32,128]{3,2,1,0:T(8,128)(2,1)}, u32[]{:S(2)}) copy-start(bf16[1,128,32,128]{3,2,1,0:T(8,128)(2,1)} %param.10) | copy-start | bytes 3145732
